TPU v7x, 32 devices: a whole 2x2x4 slice. The times are simulated.
32 devices in a mesh: group: 4 (over y, x), shard: 8 (over z, core).
Axes of the slice: x: 2, y: 2, z: 4, core: 2. Of those that a mesh axis runs over, the one named last changes fastest.
Arguments:
- queries: float32 [256, 768], P(('group', 'shard')), may hold values from -6 to 6
- codebook: float32 [96, 256, 8], replicated, may hold values from -0.21875 to 0.21875
- pq_codes: int32 [256, 96, 256], P(('group', 'shard')), may hold values from 0 to 255
- probes: int32 [256, 8], P('group'), may hold values from 0 to 63, all different within a row
- vectors: float32 [32768, 768], P(('group', 'shard')), may hold values from -0.21875 to 0.21875
- cand_owner: int32 [256, 16], P(('group', 'shard')), may hold values from 0 to 31, all different within a row; in each aligned block of 8 rows (0 to 7, 8 to 15, ...) at most 4 rows name the same one
- cand_row: int32 [256, 16], P(('group', 'shard')), may hold values from 0 to 1023
Outputs:
- pq_scores: float32 [256, 256, 64], P(('group', 'shard'))
- rerank_scores: float32 [256, 16], P(('group', 'shard'))
Inputs may be any that keep to these rules, and one draw needn't show every extreme that they name: The 8 probes of one query are distinct. `cand_owner`: the 16 owners of one query are distinct. Among the queries of one device no owner appears more than 4 times, and some owner appears exactly 4 times.
All inputs are finite; a program needn't handle non-finite values.
Results may differ from a plain program's by a relative error of at most 0.0029.
Values may be sent and summed in bfloat16 or wider, within the bound.
No kernel may reach another device: no remote copies, remote signals or barrier semaphores. Data moves between devices by JAX's collectives and lax.ppermute only.
A program may use at most 128 MiB of HBM per device.

v0:
```python
import jax
import jax.numpy as jnp
from jax import lax
from jax.sharding import PartitionSpec as P

M = 96
DS = 8
KS = 256


def build_tables(query_rows, codebook):
    number = query_rows.shape[0]
    pieces = query_rows.reshape(number, M, DS)
    tables = jnp.einsum("qmd,mkd->qmk", pieces, codebook, precision=lax.Precision.HIGHEST)
    return tables.reshape(number, M * KS).astype(jnp.bfloat16)


def score_lists(pq_codes, group_tables, probes, first_list):
    centres = jnp.arange(KS, dtype=jnp.int32)

    def one_list(inputs):
        list_codes, list_id = inputs
        onehot = (list_codes[:, None, :] == centres[None, :, None]).astype(jnp.bfloat16)
        onehot = onehot.reshape(M * KS, list_codes.shape[1])
        scores = lax.dot_general(
            onehot, group_tables, (((0,), (1,)), ((), ())), preferred_element_type=jnp.float32
        )
        probed = jnp.any(probes == list_id, axis=1)
        return jnp.where(probed[None, :], scores, 0.0)

    list_ids = first_list + jnp.arange(pq_codes.shape[0], dtype=jnp.int32)
    return lax.map(one_list, (pq_codes, list_ids))


def rerank(queries, vectors, cand_owner, cand_row):
    owners = lax.axis_size("group") * lax.axis_size("shard")
    pair_count = cand_owner.shape[0] * cand_owner.shape[1]
    capacity = max(2, pair_count // owners)
    owner_flat = cand_owner.reshape(pair_count)
    matches = (owner_flat[:, None] == jnp.arange(owners, dtype=jnp.int32)[None, :]).astype(
        jnp.int32
    )
    before = jnp.cumsum(matches, axis=0) - matches
    position = jnp.sum(before * matches, axis=1)
    target = owner_flat * capacity + position
    source = jnp.arange(pair_count, dtype=jnp.int32) // cand_owner.shape[1]
    send_rows = (
        jnp.zeros((owners * capacity, queries.shape[1]), jnp.float32)
        .at[target]
        .set(queries[source])
    )
    send_rows = send_rows.reshape(owners, capacity, queries.shape[1])
    send_ids = (
        jnp.full((owners * capacity,), -1.0, jnp.float32)
        .at[target]
        .set(cand_row.reshape(pair_count).astype(jnp.float32))
    )
    send_ids = send_ids.reshape(owners, capacity)
    rows_in = lax.all_to_all(send_rows, ("group", "shard"), split_axis=0, concat_axis=0, tiled=True)
    row_ids = lax.all_to_all(send_ids, ("group", "shard"), split_axis=0, concat_axis=0, tiled=True)
    filled = row_ids >= 0.0
    lookup = jnp.maximum(row_ids, 0.0).astype(jnp.int32)
    found = vectors[lookup]
    inner = jnp.einsum("snd,snd->sn", rows_in, found, precision=lax.Precision.HIGHEST)
    scored = jnp.where(filled, inner, 0.0)
    returned = lax.all_to_all(scored, ("group", "shard"), split_axis=0, concat_axis=0, tiled=True)
    result = returned.reshape(owners * capacity)[target]
    return result.reshape(cand_owner.shape)


def per_device(queries, codebook, pq_codes, probes, vectors, cand_owner, cand_row):
    first_list = lax.axis_index("shard") * pq_codes.shape[0]
    group_queries = lax.all_gather(queries, "shard", axis=0, tiled=True)
    group_tables = build_tables(group_queries, codebook)
    pq_scores = score_lists(pq_codes, group_tables, probes, first_list)
    rerank_scores = rerank(queries, vectors, cand_owner, cand_row)
    return (pq_scores, rerank_scores)


def solution(mesh):
    in_specs = (
        P(("group", "shard"), None),
        P(),
        P(("group", "shard"), None, None),
        P("group", None),
        P(("group", "shard"), None),
        P(("group", "shard"), None),
        P(("group", "shard"), None),
    )
    out_specs = (P(("group", "shard"), None, None), P(("group", "shard"), None))
    return jax.shard_map(
        per_device, mesh=mesh, in_specs=in_specs, out_specs=out_specs, check_vma=False
    )
```

profile of v0, /device:TPU:0, one launch (start us, length us, event | category | flops | bytes accessed | tf_op | source)
XLA Modules:
  0.0 161.3 jit_solution(348428554868212641)
XLA Ops:
  5.4 7.5 %all-to-all-start = ((f32[32,1,4]{2,1,0:T(1,128)}), f32[32,1,4]{2,1,0:T(1,128)}, u32[]{:S(2)}, u32[]{:S(2)}) async-start(f32[32,1,4]{2,1,0:T(1,128)} %bitcast.4), calls=%async_computation | async-start | bytes 32768 | tf_op jit(solution)/shard_map/all_to_all | solution.py:60
  12.8 15.7 %all_gather.3 = f32[64,768]{1,0:T(8,128)} all-gather(f32[8,768]{1,0:T(8,128)} %param.9), channel_id=1, replica_groups=mesh['group'=4,'shard'=8] {'shard'}, dimensions={0}, use_global_device_ids=true | all-gather | bytes 221184 | tf_op jit(solution)/shard_map/all_gather | solution.py:73
  29.7 7.5 %convert_bitcast_fusion = bf16[96,8,8,256]{3,2,1,0:T(8,128)(2,1)} fusion(f32[96,256,8]{1,2,0:T(8,128)} %param.10, f32[64,768]{0,1:T(8,128)S(1)} %copy.27), kind=kOutput, calls=%fused_computation.13 | convolution fusion | flops 152567808 | bytes 4128768 | tf_op jit(solution)/shard_map/qmd,mkd->qmk/dot_general | solution.py:14
  37.2 3.8 %copy.40 = bf16[96,8,8,256]{3,2,0,1:T(8,128)(2,1)} copy(bf16[96,8,8,256]{3,2,1,0:T(8,128)(2,1)} %convert_bitcast_fusion) | data formatting | bytes 6291456 | tf_op jit(solution)/shard_map/convert_element_type | solution.py:15
  44.8 5.4 %all-to-all-start.1 = ((f32[32,4,768]{2,1,0:T(4,128)}), f32[32,4,768]{2,1,0:T(4,128)S(1)}, u32[]{:S(2)}, u32[]{:S(2)}) async-start(f32[32,4,768]{2,1,0:T(4,128)} %reshape.135), calls=%async_computation.1 | async-start | bytes 786432 | tf_op jit(solution)/shard_map/all_to_all | solution.py:59
  50.3 84.8 %while.11 = (s32[]{:T(128)}, f32[8,256,64]{1,2,0:T(8,128)}, s32[8]{0:T(128)S(1)}, s32[64,8]{0,1:T(8,128)S(1)}, s32[8,96,256]{2,1,0:T(8,128)}, /*index=5*/bf16[64,24576]{1,0:T(8,128)(2,1)}, s32[]{:T(128)}) while((s32[]{:T(128)}, f32[8,256,64]{1,2,0:T(8,128)}, s32[8]{0:T(128)S(1)}, s32[64,8]{0,1:T(8,128)S(1)}, ...), condition=%wide.region_2.3_spmd.clone, body=%wide.region_0.2_spmd.clone.sunk | while | flops 811615168 | bytes 29067528 | solution.py:32
  51.5 4.3 %bitcast_compare_fusion.2 = pred[24576,256]{1,0:T(32,128)(4,1)S(1)} fusion(s32[24576]{0:T(1024)S(1)} %bitcast.56, s32[96,256]{1,0:T(8,128)S(1)} %dynamic-slice_bitcast_fusion.2), kind=kLoop, calls=%fused_computation.6.clone.1 | loop fusion | flops 6291456 | bytes 6488064 | tf_op jit(solution)/shard_map/while/body/eval_jaxpr/eq | solution.py:23
  57.0 3.9 %fusion.21 = f32[8,256,64]{1,2,0:T(8,128)} fusion(f32[8,256,64]{1,2,0:T(8,128)} %get-tuple-element.111, s32[]{:T(128)S(6)} %copy.46, pred[24576,256]{1,0:T(32,128)(4,1)S(1)} %bitcast_compare_fusion.2, bf16[64,24576]{1,0:T(8,128)(2,1)S(1)} %copy-done.1, pred[64]{0:T(512)(128)(4,1)S(1)} %compare_reduce_fusion.2), kind=kOutput, calls=%fused_computation.9.clone.1 | convolution fusion | flops 805322752 | bytes 9502788 | tf_op jit(solution)/shard_map/while/body/eval_jaxpr/dot_general | solution.py:25
  62.1 4.3 %bitcast_compare_fusion.2 = pred[24576,256]{1,0:T(32,128)(4,1)S(1)} fusion(s32[24576]{0:T(1024)S(1)} %bitcast.56, s32[96,256]{1,0:T(8,128)S(1)} %dynamic-slice_bitcast_fusion.2), kind=kLoop, calls=%fused_computation.6.clone.1 | loop fusion | flops 6291456 | bytes 6488064 | tf_op jit(solution)/shard_map/while/body/eval_jaxpr/eq | solution.py:23
  67.6 3.9 %fusion.21 = f32[8,256,64]{1,2,0:T(8,128)} fusion(f32[8,256,64]{1,2,0:T(8,128)} %get-tuple-element.111, s32[]{:T(128)S(6)} %copy.46, pred[24576,256]{1,0:T(32,128)(4,1)S(1)} %bitcast_compare_fusion.2, bf16[64,24576]{1,0:T(8,128)(2,1)S(1)} %copy-done.1, pred[64]{0:T(512)(128)(4,1)S(1)} %compare_reduce_fusion.2), kind=kOutput, calls=%fused_computation.9.clone.1 | convolution fusion | flops 805322752 | bytes 9502788 | tf_op jit(solution)/shard_map/while/body/eval_jaxpr/dot_general | solution.py:25
  72.7 4.3 %bitcast_compare_fusion.2 = pred[24576,256]{1,0:T(32,128)(4,1)S(1)} fusion(s32[24576]{0:T(1024)S(1)} %bitcast.56, s32[96,256]{1,0:T(8,128)S(1)} %dynamic-slice_bitcast_fusion.2), kind=kLoop, calls=%fused_computation.6.clone.1 | loop fusion | flops 6291456 | bytes 6488064 | tf_op jit(solution)/shard_map/while/body/eval_jaxpr/eq | solution.py:23
  78.2 3.9 %fusion.21 = f32[8,256,64]{1,2,0:T(8,128)} fusion(f32[8,256,64]{1,2,0:T(8,128)} %get-tuple-element.111, s32[]{:T(128)S(6)} %copy.46, pred[24576,256]{1,0:T(32,128)(4,1)S(1)} %bitcast_compare_fusion.2, bf16[64,24576]{1,0:T(8,128)(2,1)S(1)} %copy-done.1, pred[64]{0:T(512)(128)(4,1)S(1)} %compare_reduce_fusion.2), kind=kOutput, calls=%fused_computation.9.clone.1 | convolution fusion | flops 805322752 | bytes 9502788 | tf_op jit(solution)/shard_map/while/body/eval_jaxpr/dot_general | solution.py:25
  83.3 4.3 %bitcast_compare_fusion.2 = pred[24576,256]{1,0:T(32,128)(4,1)S(1)} fusion(s32[24576]{0:T(1024)S(1)} %bitcast.56, s32[96,256]{1,0:T(8,128)S(1)} %dynamic-slice_bitcast_fusion.2), kind=kLoop, calls=%fused_computation.6.clone.1 | loop fusion | flops 6291456 | bytes 6488064 | tf_op jit(solution)/shard_map/while/body/eval_jaxpr/eq | solution.py:23
  88.8 3.9 %fusion.21 = f32[8,256,64]{1,2,0:T(8,128)} fusion(f32[8,256,64]{1,2,0:T(8,128)} %get-tuple-element.111, s32[]{:T(128)S(6)} %copy.46, pred[24576,256]{1,0:T(32,128)(4,1)S(1)} %bitcast_compare_fusion.2, bf16[64,24576]{1,0:T(8,128)(2,1)S(1)} %copy-done.1, pred[64]{0:T(512)(128)(4,1)S(1)} %compare_reduce_fusion.2), kind=kOutput, calls=%fused_computation.9.clone.1 | convolution fusion | flops 805322752 | bytes 9502788 | tf_op jit(solution)/shard_map/while/body/eval_jaxpr/dot_general | solution.py:25
  93.8 4.3 %bitcast_compare_fusion.2 = pred[24576,256]{1,0:T(32,128)(4,1)S(1)} fusion(s32[24576]{0:T(1024)S(1)} %bitcast.56, s32[96,256]{1,0:T(8,128)S(1)} %dynamic-slice_bitcast_fusion.2), kind=kLoop, calls=%fused_computation.6.clone.1 | loop fusion | flops 6291456 | bytes 6488064 | tf_op jit(solution)/shard_map/while/body/eval_jaxpr/eq | solution.py:23
  99.4 3.9 %fusion.21 = f32[8,256,64]{1,2,0:T(8,128)} fusion(f32[8,256,64]{1,2,0:T(8,128)} %get-tuple-element.111, s32[]{:T(128)S(6)} %copy.46, pred[24576,256]{1,0:T(32,128)(4,1)S(1)} %bitcast_compare_fusion.2, bf16[64,24576]{1,0:T(8,128)(2,1)S(1)} %copy-done.1, pred[64]{0:T(512)(128)(4,1)S(1)} %compare_reduce_fusion.2), kind=kOutput, calls=%fused_computation.9.clone.1 | convolution fusion | flops 805322752 | bytes 9502788 | tf_op jit(solution)/shard_map/while/body/eval_jaxpr/dot_general | solution.py:25
  104.4 4.3 %bitcast_compare_fusion.2 = pred[24576,256]{1,0:T(32,128)(4,1)S(1)} fusion(s32[24576]{0:T(1024)S(1)} %bitcast.56, s32[96,256]{1,0:T(8,128)S(1)} %dynamic-slice_bitcast_fusion.2), kind=kLoop, calls=%fused_computation.6.clone.1 | loop fusion | flops 6291456 | bytes 6488064 | tf_op jit(solution)/shard_map/while/body/eval_jaxpr/eq | solution.py:23
  110.0 3.9 %fusion.21 = f32[8,256,64]{1,2,0:T(8,128)} fusion(f32[8,256,64]{1,2,0:T(8,128)} %get-tuple-element.111, s32[]{:T(128)S(6)} %copy.46, pred[24576,256]{1,0:T(32,128)(4,1)S(1)} %bitcast_compare_fusion.2, bf16[64,24576]{1,0:T(8,128)(2,1)S(1)} %copy-done.1, pred[64]{0:T(512)(128)(4,1)S(1)} %compare_reduce_fusion.2), kind=kOutput, calls=%fused_computation.9.clone.1 | convolution fusion | flops 805322752 | bytes 9502788 | tf_op jit(solution)/shard_map/while/body/eval_jaxpr/dot_general | solution.py:25
  115.0 4.3 %bitcast_compare_fusion.2 = pred[24576,256]{1,0:T(32,128)(4,1)S(1)} fusion(s32[24576]{0:T(1024)S(1)} %bitcast.56, s32[96,256]{1,0:T(8,128)S(1)} %dynamic-slice_bitcast_fusion.2), kind=kLoop, calls=%fused_computation.6.clone.1 | loop fusion | flops 6291456 | bytes 6488064 | tf_op jit(solution)/shard_map/while/body/eval_jaxpr/eq | solution.py:23
  120.6 3.9 %fusion.21 = f32[8,256,64]{1,2,0:T(8,128)} fusion(f32[8,256,64]{1,2,0:T(8,128)} %get-tuple-element.111, s32[]{:T(128)S(6)} %copy.46, pred[24576,256]{1,0:T(32,128)(4,1)S(1)} %bitcast_compare_fusion.2, bf16[64,24576]{1,0:T(8,128)(2,1)S(1)} %copy-done.1, pred[64]{0:T(512)(128)(4,1)S(1)} %compare_reduce_fusion.2), kind=kOutput, calls=%fused_computation.9.clone.1 | convolution fusion | flops 805322752 | bytes 9502788 | tf_op jit(solution)/shard_map/while/body/eval_jaxpr/dot_general | solution.py:25
  125.6 4.3 %bitcast_compare_fusion.2 = pred[24576,256]{1,0:T(32,128)(4,1)S(1)} fusion(s32[24576]{0:T(1024)S(1)} %bitcast.56, s32[96,256]{1,0:T(8,128)S(1)} %dynamic-slice_bitcast_fusion.2), kind=kLoop, calls=%fused_computation.6.clone.1 | loop fusion | flops 6291456 | bytes 6488064 | tf_op jit(solution)/shard_map/while/body/eval_jaxpr/eq | solution.py:23
  131.2 3.9 %fusion.21 = f32[8,256,64]{1,2,0:T(8,128)} fusion(f32[8,256,64]{1,2,0:T(8,128)} %get-tuple-element.111, s32[]{:T(128)S(6)} %copy.46, pred[24576,256]{1,0:T(32,128)(4,1)S(1)} %bitcast_compare_fusion.2, bf16[64,24576]{1,0:T(8,128)(2,1)S(1)} %copy-done.1, pred[64]{0:T(512)(128)(4,1)S(1)} %compare_reduce_fusion.2), kind=kOutput, calls=%fused_computation.9.clone.1 | convolution fusion | flops 805322752 | bytes 9502788 | tf_op jit(solution)/shard_map/while/body/eval_jaxpr/dot_general | solution.py:25
  145.1 5.8 %all-to-all-start.2 = ((f32[32,1,4]{2,1,0:T(1,128)}), f32[32,1,4]{2,1,0:T(1,128)S(1)}, u32[]{:S(2)}, u32[]{:S(2)}) async-start(f32[32,1,4]{2,1,0:T(1,128)} %copy.33), calls=%async_computation.2 | async-start | bytes 32768 | tf_op jit(solution)/shard_map/all_to_all | solution.py:66
  151.6 6.5 %all-to-all-done.2 = f32[32,1,4]{2,1,0:T(1,128)S(1)} async-done(((f32[32,1,4]{2,1,0:T(1,128)}), f32[32,1,4]{2,1,0:T(1,128)S(1)}, u32[]{:S(2)}, u32[]{:S(2)}) %all-to-all-start.2) | async-done | bytes 544 | tf_op jit(solution)/shard_map/all_to_all | solution.py:66
  (101 shorter events, 42.7 us)
Async XLA Ops:
  0.6 138.5 %copy-start = (f32[1024,768]{1,0:T(8,128)S(1)}, f32[1024,768]{1,0:T(8,128)}, u32[]{:S(2)}) copy-start(f32[1024,768]{1,0:T(8,128)} %param.13) | copy-start | bytes 9437188
  3.7 41.2 %copy-start.4 = (s32[128]{0:T(128)}, s32[128]{0:T(128)S(1)}, u32[]{:S(2)}) copy-start(s32[128]{0:T(128)S(1)} %fusion.10) | copy-start | bytes 1540
  5.4 39.5 %all-to-all-start = ((f32[32,1,4]{2,1,0:T(1,128)}), f32[32,1,4]{2,1,0:T(1,128)}, u32[]{:S(2)}, u32[]{:S(2)}) async-start(f32[32,1,4]{2,1,0:T(1,128)} %bitcast.4), calls=%async_computation | async-start | bytes 32768 | tf_op jit(solution)/shard_map/all_to_all | solution.py:60
  29.7 20.6 %copy-start.2 = (s32[64,8]{0,1:T(8,128)S(1)}, s32[64,8]{0,1:T(8,128)}, u32[]{:S(2)}) copy-start(s32[64,8]{0,1:T(8,128)} %param.12) | copy-start | bytes 6148
  44.8 97.7 %all-to-all-start.1 = ((f32[32,4,768]{2,1,0:T(4,128)}), f32[32,4,768]{2,1,0:T(4,128)S(1)}, u32[]{:S(2)}, u32[]{:S(2)}) async-start(f32[32,4,768]{2,1,0:T(4,128)} %reshape.135), calls=%async_computation.1 | async-start | bytes 786432 | tf_op jit(solution)/shard_map/all_to_all | solution.py:59
  50.3 6.7 %copy-start.1 = (bf16[64,24576]{1,0:T(8,128)(2,1)S(1)}, bf16[64,24576]{1,0:T(8,128)(2,1)}, u32[]{:S(2)}) copy-start(bf16[64,24576]{1,0:T(8,128)(2,1)} %get-tuple-element.122) | copy-start | bytes 9437188 | tf_op jit(solution)/shard_map/while
  60.9 6.7 %copy-start.1 = (bf16[64,24576]{1,0:T(8,128)(2,1)S(1)}, bf16[64,24576]{1,0:T(8,128)(2,1)}, u32[]{:S(2)}) copy-start(bf16[64,24576]{1,0:T(8,128)(2,1)} %get-tuple-element.122) | copy-start | bytes 9437188 | tf_op jit(solution)/shard_map/while
  71.5 6.7 %copy-start.1 = (bf16[64,24576]{1,0:T(8,128)(2,1)S(1)}, bf16[64,24576]{1,0:T(8,128)(2,1)}, u32[]{:S(2)}) copy-start(bf16[64,24576]{1,0:T(8,128)(2,1)} %get-tuple-element.122) | copy-start | bytes 9437188 | tf_op jit(solution)/shard_map/while
  82.1 6.7 %copy-start.1 = (bf16[64,24576]{1,0:T(8,128)(2,1)S(1)}, bf16[64,24576]{1,0:T(8,128)(2,1)}, u32[]{:S(2)}) copy-start(bf16[64,24576]{1,0:T(8,128)(2,1)} %get-tuple-element.122) | copy-start | bytes 9437188 | tf_op jit(solution)/shard_map/while
  92.7 6.7 %copy-start.1 = (bf16[64,24576]{1,0:T(8,128)(2,1)S(1)}, bf16[64,24576]{1,0:T(8,128)(2,1)}, u32[]{:S(2)}) copy-start(bf16[64,24576]{1,0:T(8,128)(2,1)} %get-tuple-element.122) | copy-start | bytes 9437188 | tf_op jit(solution)/shard_map/while
  103.3 6.7 %copy-start.1 = (bf16[64,24576]{1,0:T(8,128)(2,1)S(1)}, bf16[64,24576]{1,0:T(8,128)(2,1)}, u32[]{:S(2)}) copy-start(bf16[64,24576]{1,0:T(8,128)(2,1)} %get-tuple-element.122) | copy-start | bytes 9437188 | tf_op jit(solution)/shard_map/while
  113.9 6.7 %copy-start.1 = (bf16[64,24576]{1,0:T(8,128)(2,1)S(1)}, bf16[64,24576]{1,0:T(8,128)(2,1)}, u32[]{:S(2)}) copy-start(bf16[64,24576]{1,0:T(8,128)(2,1)} %get-tuple-element.122) | copy-start | bytes 9437188 | tf_op jit(solution)/shard_map/while
  124.5 6.7 %copy-start.1 = (bf16[64,24576]{1,0:T(8,128)(2,1)S(1)}, bf16[64,24576]{1,0:T(8,128)(2,1)}, u32[]{:S(2)}) copy-start(bf16[64,24576]{1,0:T(8,128)(2,1)} %get-tuple-element.122) | copy-start | bytes 9437188 | tf_op jit(solution)/shard_map/while
  135.9 0.6 copy-start.3
  145.1 13.0 %all-to-all-start.2 = ((f32[32,1,4]{2,1,0:T(1,128)}), f32[32,1,4]{2,1,0:T(1,128)S(1)}, u32[]{:S(2)}, u32[]{:S(2)}) async-start(f32[32,1,4]{2,1,0:T(1,128)} %copy.33), calls=%async_computation.2 | async-start | bytes 32768 | tf_op jit(solution)/shard_map/all_to_all | solution.py:66
where the time goes:
time: 162 us; the launch traced here: 161 us
  other arithmetic  45.8 us (28%)
  matrix products  38.9 us (24%)
  local copies, waits for them, and re-layouts  34.8 us (21%)
  starting transfers between devices  18.7 us (12%)
  blocking collectives  15.7 us (10%)
  waiting for transfers between devices  6.5 us (4%)
    eq x8, other arithmetic, one_list(): list_codes[:, None, :] == centres[None, :, None]  34.1 us
    dot_general x8, matrix products, one_list(): lax.dot_general(onehot, group_tables, (((0,), (1,)), ((), ())), preferred...  31.3 us
    all_gather x1, blocking collectives, per_device(): group_queries = lax.all_gather(queries, 'shard', axis=0, tiled=True)  15.7 us
    eq x8, local copies, waits for them, and re-layouts, one_list(): list_codes[:, None, :] == centres[None, :, None]  8.45 us
    dot_general x1, matrix products, build_tables(): jnp.einsum('qmd,mkd->qmk', pieces, codebook, precision=lax.Precision.HIGH...  7.55 us
    all_to_all x1, starting transfers between devices, rerank(): lax.all_to_all(send_ids, ('group', 'shard'), split_axis=0, concat_axis=0,...  7.45 us
    all_to_all x1, waiting for transfers between devices, rerank(): lax.all_to_all(scored, ('group', 'shard'), split_axis=0, concat_axis=0, t...  6.49 us
    all_to_all x1, starting transfers between devices, rerank(): lax.all_to_all(scored, ('group', 'shard'), split_axis=0, concat_axis=0, t...  5.83 us
  transfers between devices with their start and end apart: 3, of which 1 were waited for; matrix products, arithmetic and copies ran while one was open for 67% of the time, Pallas kernels for 0%

commit v1 on v0

--- a/solution.py
+++ b/solution.py
@@ -70,7 +70,17 @@
 
 def per_device(queries, codebook, pq_codes, probes, vectors, cand_owner, cand_row):
     first_list = lax.axis_index("shard") * pq_codes.shape[0]
-    group_queries = lax.all_gather(queries, "shard", axis=0, tiled=True)
+    made = [queries]
+    n_slots = lax.axis_size("shard")
+    for src_i in range(n_slots - 1):
+        made.append(
+            lax.ppermute(made[-1], "shard", [(p, (p + 1) % n_slots) for p in range(n_slots)])
+        )
+    group_queries = jnp.roll(
+        jnp.concatenate(made[::-1], axis=0),
+        shift=(lax.axis_index("shard") + 1) * queries.shape[0],
+        axis=0,
+    )
     group_tables = build_tables(group_queries, codebook)
     pq_scores = score_lists(pq_codes, group_tables, probes, first_list)
     rerank_scores = rerank(queries, vectors, cand_owner, cand_row)

time: 162 us -> 172 us (1.062)
  waiting for transfers between devices: 6.5 us -> 22.7 us
  blocking collectives: 15.7 us -> 0 us
  local copies, waits for them, and re-layouts: 34.8 us -> 43.5 us
    ppermute x0 -> x7, waiting for transfers between devices: none -> 22.7 us  [per_device(): lax.ppermute(made[-1], 'shard', [(p, (p + 1) % n_slots) for p in range(n_...]
    all_gather x1 -> x0, blocking collectives: 15.7 us -> none  [per_device(): group_queries = lax.all_gather(queries, 'shard', axis=0, tiled=True)]
    unnamed x8 -> x33, local copies, waits for them, and re-layouts: 0.61 us -> 11.1 us
    all_to_all x1, waiting for transfers between devices: 6.49 us -> 0.01 us  [rerank(): lax.all_to_all(scored, ('group', 'shard'), split_axis=0, concat_axis=0, t...]
    dynamic_slice x0 -> x2, local copies, waits for them, and re-layouts: none -> 2.55 us  [per_device(): jnp.roll(jnp.concatenate(made[::-1], axis=0), shift=(lax.axis_index('shar...]
    convert_element_type x1, local copies, waits for them, and re-layouts: 3.76 us -> 1.85 us  [build_tables(): return tables.reshape(number, M * KS).astype(jnp.bfloat16)]
    reduce_or x8, other arithmetic: 5.23 us -> 6.95 us  [one_list(): probed = jnp.any(probes == list_id, axis=1)]
  transfers between devices with their start and end apart: 3 -> 10, of which waited for: 1 -> 5; matrix products, arithmetic and copies ran while one was open for 67% -> 71% of each run, Pallas kernels for 0% -> 0%
where the time goes in v1:
time: 172 us; the launch traced here: 171 us
  other arithmetic  46.4 us (27%)
  local copies, waits for them, and re-layouts  43.5 us (25%)
  matrix products  37.7 us (22%)
  waiting for transfers between devices  22.7 us (13%)
  starting transfers between devices  19.3 us (11%)
    eq x8, other arithmetic, one_list(): list_codes[:, None, :] == centres[None, :, None]  34.6 us
    dot_general x8, matrix products, one_list(): lax.dot_general(onehot, group_tables, (((0,), (1,)), ((), ())), preferred...  31.3 us
    ppermute x7, waiting for transfers between devices, per_device(): lax.ppermute(made[-1], 'shard', [(p, (p + 1) % n_slots) for p in range(n_...  22.7 us
    unnamed x33, local copies, waits for them, and re-layouts  11.1 us
    eq x8, local copies, waits for them, and re-layouts, one_list(): list_codes[:, None, :] == centres[None, :, None]  7.22 us
    reduce_or x8, other arithmetic, one_list(): probed = jnp.any(probes == list_id, axis=1)  6.95 us
    dot_general x1, matrix products, build_tables(): jnp.einsum('qmd,mkd->qmk', pieces, codebook, precision=lax.Precision.HIGH...  6.36 us
    all_to_all x1, starting transfers between devices, rerank(): lax.all_to_all(send_ids, ('group', 'shard'), split_axis=0, concat_axis=0,...  6.27 us
  transfers between devices with their start and end apart: 10, of which 5 were waited for; matrix products, arithmetic and copies ran while one was open for 71% of the time, Pallas kernels for 0%

profile of v1, /device:TPU:0, one launch (start us, length us, event | category | flops | bytes accessed | tf_op | source)
XLA Modules:
  0.0 170.6 jit_solution(16261544470545428488)
XLA Ops:
  9.4 6.3 %all-to-all-start = ((f32[32,1,4]{2,1,0:T(1,128)}), f32[32,1,4]{2,1,0:T(1,128)S(1)}, u32[]{:S(2)}, u32[]{:S(2)}) async-start(f32[32,1,4]{2,1,0:T(1,128)} %bitcast.4), calls=%async_computation | async-start | bytes 32768 | tf_op jit(solution)/shard_map/all_to_all | solution.py:60
  16.0 4.8 %collective-permute-done.2 = f32[8,768]{1,0:T(8,128)S(1)} collective-permute-done((f32[8,768]{1,0:T(8,128)S(1)}, f32[8,768]{1,0:T(8,128)S(1)}, u32[]{:S(2)}, u32[]{:S(2)}) %collective-permute-start.2) | collective-permute-done | bytes 24608 | tf_op jit(solution)/shard_map/ppermute | solution.py:77
  20.9 5.0 %collective-permute-done.3 = f32[8,768]{1,0:T(8,128)S(1)} collective-permute-done((f32[8,768]{1,0:T(8,128)S(1)}, f32[8,768]{1,0:T(8,128)S(1)}, u32[]{:S(2)}, u32[]{:S(2)}) %collective-permute-start.3) | collective-permute-done | bytes 24608 | tf_op jit(solution)/shard_map/ppermute | solution.py:77
  26.6 4.4 %collective-permute-done.4 = f32[8,768]{1,0:T(8,128)S(1)} collective-permute-done((f32[8,768]{1,0:T(8,128)S(1)}, f32[8,768]{1,0:T(8,128)S(1)}, u32[]{:S(2)}, u32[]{:S(2)}) %collective-permute-start.4) | collective-permute-done | bytes 24608 | tf_op jit(solution)/shard_map/ppermute | solution.py:77
  31.2 4.9 %collective-permute-done.5 = f32[8,768]{1,0:T(8,128)} collective-permute-done((f32[8,768]{1,0:T(8,128)S(1)}, f32[8,768]{1,0:T(8,128)}, u32[]{:S(2)}, u32[]{:S(2)}) %collective-permute-start.5) | collective-permute-done | bytes 24608 | tf_op jit(solution)/shard_map/ppermute | solution.py:77
  40.4 6.1 %all-to-all-start.1 = ((f32[32,4,768]{2,1,0:T(4,128)}), f32[32,4,768]{2,1,0:T(4,128)S(1)}, u32[]{:S(2)}, u32[]{:S(2)}) async-start(f32[32,4,768]{2,1,0:T(4,128)} %reshape.135), calls=%async_computation.1 | async-start | bytes 786432 | tf_op jit(solution)/shard_map/all_to_all | solution.py:59
  64.4 6.4 %convert_bitcast_fusion = bf16[96,8,8,256]{3,2,1,0:T(8,128)(2,1)S(1)} fusion(f32[96,256,8]{1,2,0:T(8,128)} %param.10, f32[64,768]{0,1:T(8,128)} %copy.27), kind=kOutput, calls=%fused_computation.13 | convolution fusion | flops 152567808 | bytes 4128768 | tf_op jit(solution)/shard_map/qmd,mkd->qmk/dot_general | solution.py:14
  75.9 6.0 %all-to-all-start.2 = ((f32[32,1,4]{2,1,0:T(1,128)}), f32[32,1,4]{2,1,0:T(1,128)S(1)}, u32[]{:S(2)}, u32[]{:S(2)}) async-start(f32[32,1,4]{2,1,0:T(1,128)} %copy.33), calls=%async_computation.2 | async-start | bytes 32768 | tf_op jit(solution)/shard_map/all_to_all | solution.py:66
  81.9 85.5 %while.11 = (s32[]{:T(128)}, f32[8,256,64]{1,2,0:T(8,128)}, s32[8]{0:T(128)S(1)}, s32[64,8]{0,1:T(8,128)S(1)}, s32[8,96,256]{2,1,0:T(8,128)}, /*index=5*/bf16[64,24576]{1,0:T(8,128)(2,1)}, s32[]{:T(128)}) while((s32[]{:T(128)}, f32[8,256,64]{1,2,0:T(8,128)}, s32[8]{0:T(128)S(1)}, s32[64,8]{0,1:T(8,128)S(1)}, ...), condition=%wide.region_2.3_spmd.clone, body=%wide.region_0.2_spmd.clone.sunk | while | flops 811615168 | bytes 29068028 | solution.py:32
  84.4 4.3 %bitcast_compare_fusion.2 = pred[24576,256]{1,0:T(32,128)(4,1)S(1)} fusion(s32[24576]{0:T(1024)S(1)} %bitcast.56, s32[96,256]{1,0:T(8,128)S(1)} %dynamic-slice_bitcast_fusion.2), kind=kLoop, calls=%fused_computation.6.clone.1 | loop fusion | flops 6291456 | bytes 6488064 | tf_op jit(solution)/shard_map/while/body/eval_jaxpr/eq | solution.py:23
  88.7 3.9 %fusion.21 = f32[8,256,64]{1,2,0:T(8,128)} fusion(f32[8,256,64]{1,2,0:T(8,128)} %get-tuple-element.113, s32[]{:T(128)} %get-tuple-element.112, pred[24576,256]{1,0:T(32,128)(4,1)S(1)} %bitcast_compare_fusion.2, bf16[64,24576]{1,0:T(8,128)(2,1)S(1)} %copy-done.1, pred[64]{0:T(512)(128)(4,1)S(1)} %compare_reduce_fusion.2), kind=kOutput, calls=%fused_computation.9.clone.1 | convolution fusion | flops 805322752 | bytes 9503296 | tf_op jit(solution)/shard_map/while/body/eval_jaxpr/dot_general | solution.py:25
  95.0 4.3 %bitcast_compare_fusion.2 = pred[24576,256]{1,0:T(32,128)(4,1)S(1)} fusion(s32[24576]{0:T(1024)S(1)} %bitcast.56, s32[96,256]{1,0:T(8,128)S(1)} %dynamic-slice_bitcast_fusion.2), kind=kLoop, calls=%fused_computation.6.clone.1 | loop fusion | flops 6291456 | bytes 6488064 | tf_op jit(solution)/shard_map/while/body/eval_jaxpr/eq | solution.py:23
  99.4 3.9 %fusion.21 = f32[8,256,64]{1,2,0:T(8,128)} fusion(f32[8,256,64]{1,2,0:T(8,128)} %get-tuple-element.113, s32[]{:T(128)} %get-tuple-element.112, pred[24576,256]{1,0:T(32,128)(4,1)S(1)} %bitcast_compare_fusion.2, bf16[64,24576]{1,0:T(8,128)(2,1)S(1)} %copy-done.1, pred[64]{0:T(512)(128)(4,1)S(1)} %compare_reduce_fusion.2), kind=kOutput, calls=%fused_computation.9.clone.1 | convolution fusion | flops 805322752 | bytes 9503296 | tf_op jit(solution)/shard_map/while/body/eval_jaxpr/dot_general | solution.py:25
  105.7 4.3 %bitcast_compare_fusion.2 = pred[24576,256]{1,0:T(32,128)(4,1)S(1)} fusion(s32[24576]{0:T(1024)S(1)} %bitcast.56, s32[96,256]{1,0:T(8,128)S(1)} %dynamic-slice_bitcast_fusion.2), kind=kLoop, calls=%fused_computation.6.clone.1 | loop fusion | flops 6291456 | bytes 6488064 | tf_op jit(solution)/shard_map/while/body/eval_jaxpr/eq | solution.py:23
  110.1 3.9 %fusion.21 = f32[8,256,64]{1,2,0:T(8,128)} fusion(f32[8,256,64]{1,2,0:T(8,128)} %get-tuple-element.113, s32[]{:T(128)} %get-tuple-element.112, pred[24576,256]{1,0:T(32,128)(4,1)S(1)} %bitcast_compare_fusion.2, bf16[64,24576]{1,0:T(8,128)(2,1)S(1)} %copy-done.1, pred[64]{0:T(512)(128)(4,1)S(1)} %compare_reduce_fusion.2), kind=kOutput, calls=%fused_computation.9.clone.1 | convolution fusion | flops 805322752 | bytes 9503296 | tf_op jit(solution)/shard_map/while/body/eval_jaxpr/dot_general | solution.py:25
  116.4 4.3 %bitcast_compare_fusion.2 = pred[24576,256]{1,0:T(32,128)(4,1)S(1)} fusion(s32[24576]{0:T(1024)S(1)} %bitcast.56, s32[96,256]{1,0:T(8,128)S(1)} %dynamic-slice_bitcast_fusion.2), kind=kLoop, calls=%fused_computation.6.clone.1 | loop fusion | flops 6291456 | bytes 6488064 | tf_op jit(solution)/shard_map/while/body/eval_jaxpr/eq | solution.py:23
  120.7 3.9 %fusion.21 = f32[8,256,64]{1,2,0:T(8,128)} fusion(f32[8,256,64]{1,2,0:T(8,128)} %get-tuple-element.113, s32[]{:T(128)} %get-tuple-element.112, pred[24576,256]{1,0:T(32,128)(4,1)S(1)} %bitcast_compare_fusion.2, bf16[64,24576]{1,0:T(8,128)(2,1)S(1)} %copy-done.1, pred[64]{0:T(512)(128)(4,1)S(1)} %compare_reduce_fusion.2), kind=kOutput, calls=%fused_computation.9.clone.1 | convolution fusion | flops 805322752 | bytes 9503296 | tf_op jit(solution)/shard_map/while/body/eval_jaxpr/dot_general | solution.py:25
  127.1 4.3 %bitcast_compare_fusion.2 = pred[24576,256]{1,0:T(32,128)(4,1)S(1)} fusion(s32[24576]{0:T(1024)S(1)} %bitcast.56, s32[96,256]{1,0:T(8,128)S(1)} %dynamic-slice_bitcast_fusion.2), kind=kLoop, calls=%fused_computation.6.clone.1 | loop fusion | flops 6291456 | bytes 6488064 | tf_op jit(solution)/shard_map/while/body/eval_jaxpr/eq | solution.py:23
  131.4 3.9 %fusion.21 = f32[8,256,64]{1,2,0:T(8,128)} fusion(f32[8,256,64]{1,2,0:T(8,128)} %get-tuple-element.113, s32[]{:T(128)} %get-tuple-element.112, pred[24576,256]{1,0:T(32,128)(4,1)S(1)} %bitcast_compare_fusion.2, bf16[64,24576]{1,0:T(8,128)(2,1)S(1)} %copy-done.1, pred[64]{0:T(512)(128)(4,1)S(1)} %compare_reduce_fusion.2), kind=kOutput, calls=%fused_computation.9.clone.1 | convolution fusion | flops 805322752 | bytes 9503296 | tf_op jit(solution)/shard_map/while/body/eval_jaxpr/dot_general | solution.py:25
  137.8 4.3 %bitcast_compare_fusion.2 = pred[24576,256]{1,0:T(32,128)(4,1)S(1)} fusion(s32[24576]{0:T(1024)S(1)} %bitcast.56, s32[96,256]{1,0:T(8,128)S(1)} %dynamic-slice_bitcast_fusion.2), kind=kLoop, calls=%fused_computation.6.clone.1 | loop fusion | flops 6291456 | bytes 6488064 | tf_op jit(solution)/shard_map/while/body/eval_jaxpr/eq | solution.py:23
  148.5 4.3 %bitcast_compare_fusion.2 = pred[24576,256]{1,0:T(32,128)(4,1)S(1)} fusion(s32[24576]{0:T(1024)S(1)} %bitcast.56, s32[96,256]{1,0:T(8,128)S(1)} %dynamic-slice_bitcast_fusion.2), kind=kLoop, calls=%fused_computation.6.clone.1 | loop fusion | flops 6291456 | bytes 6488064 | tf_op jit(solution)/shard_map/while/body/eval_jaxpr/eq | solution.py:23
  152.8 3.9 %fusion.21 = f32[8,256,64]{1,2,0:T(8,128)} fusion(f32[8,256,64]{1,2,0:T(8,128)} %get-tuple-element.113, s32[]{:T(128)} %get-tuple-element.112, pred[24576,256]{1,0:T(32,128)(4,1)S(1)} %bitcast_compare_fusion.2, bf16[64,24576]{1,0:T(8,128)(2,1)S(1)} %copy-done.1, pred[64]{0:T(512)(128)(4,1)S(1)} %compare_reduce_fusion.2), kind=kOutput, calls=%fused_computation.9.clone.1 | convolution fusion | flops 805322752 | bytes 9503296 | tf_op jit(solution)/shard_map/while/body/eval_jaxpr/dot_general | solution.py:25
  159.1 4.3 %bitcast_compare_fusion.2 = pred[24576,256]{1,0:T(32,128)(4,1)S(1)} fusion(s32[24576]{0:T(1024)S(1)} %bitcast.56, s32[96,256]{1,0:T(8,128)S(1)} %dynamic-slice_bitcast_fusion.2), kind=kLoop, calls=%fused_computation.6.clone.1 | loop fusion | flops 6291456 | bytes 6488064 | tf_op jit(solution)/shard_map/while/body/eval_jaxpr/eq | solution.py:23
  163.5 3.9 %fusion.21 = f32[8,256,64]{1,2,0:T(8,128)} fusion(f32[8,256,64]{1,2,0:T(8,128)} %get-tuple-element.113, s32[]{:T(128)} %get-tuple-element.112, pred[24576,256]{1,0:T(32,128)(4,1)S(1)} %bitcast_compare_fusion.2, bf16[64,24576]{1,0:T(8,128)(2,1)S(1)} %copy-done.1, pred[64]{0:T(512)(128)(4,1)S(1)} %compare_reduce_fusion.2), kind=kOutput, calls=%fused_computation.9.clone.1 | convolution fusion | flops 805322752 | bytes 9503296 | tf_op jit(solution)/shard_map/while/body/eval_jaxpr/dot_general | solution.py:25
  (140 shorter events, 63.6 us)
Async XLA Ops:
  0.6 45.9 %copy-start = (f32[1024,768]{1,0:T(8,128)S(1)}, f32[1024,768]{1,0:T(8,128)}, u32[]{:S(2)}) copy-start(f32[1024,768]{1,0:T(8,128)} %param.13) | copy-start | bytes 9437188
  0.6 6.3 %collective-permute-start = (f32[8,768]{1,0:T(8,128)}, f32[8,768]{1,0:T(8,128)S(1)}, u32[]{:S(2)}, u32[]{:S(2)}) collective-permute-start(f32[8,768]{1,0:T(8,128)} %param.9), channel_id=1, source_target_pairs={{0,1},{1,2},{2,3},{3,4},{4,5},{5,6},{6,7},{7,0},{8,9},{9,10},{10,1... | collective-permute-start | bytes 73736 | tf_op jit(solution)/shard_map/ppermute | solution.py:77
  6.9 29.2 %copy-start.3 = (f32[8,768]{1,0:T(8,128)}, f32[8,768]{1,0:T(8,128)S(1)}, u32[]{:S(2)}) copy-start(f32[8,768]{1,0:T(8,128)S(1)} %collective-permute-done) | copy-start | bytes 73732
  6.9 8.8 %collective-permute-start.1 = (f32[8,768]{1,0:T(8,128)S(1)}, f32[8,768]{1,0:T(8,128)S(1)}, u32[]{:S(2)}, u32[]{:S(2)}) collective-permute-start(f32[8,768]{1,0:T(8,128)S(1)} %collective-permute-done), channel_id=1, source_target_pairs={{0,1},{1,2},{2,3},{3,4},{4,5},{5,6},{6,7},{7,0},{8,9},{9,10},{10,1... | collective-permute-start | bytes 73736 | tf_op jit(solution)/shard_map/ppermute | solution.py:77
  7.0 24.0 %copy-start.8 = (s32[128]{0:T(128)}, s32[128]{0:T(128)S(1)}, u32[]{:S(2)}) copy-start(s32[128]{0:T(128)S(1)} %fusion.10) | copy-start | bytes 1540
  9.4 17.1 %all-to-all-start = ((f32[32,1,4]{2,1,0:T(1,128)}), f32[32,1,4]{2,1,0:T(1,128)S(1)}, u32[]{:S(2)}, u32[]{:S(2)}) async-start(f32[32,1,4]{2,1,0:T(1,128)} %bitcast.4), calls=%async_computation | async-start | bytes 32768 | tf_op jit(solution)/shard_map/all_to_all | solution.py:60
  15.7 20.4 %copy-start.4 = (f32[8,768]{1,0:T(8,128)}, f32[8,768]{1,0:T(8,128)S(1)}, u32[]{:S(2)}) copy-start(f32[8,768]{1,0:T(8,128)S(1)} %collective-permute-done.1) | copy-start | bytes 73732
  15.7 5.1 %collective-permute-start.2 = (f32[8,768]{1,0:T(8,128)S(1)}, f32[8,768]{1,0:T(8,128)S(1)}, u32[]{:S(2)}, u32[]{:S(2)}) collective-permute-start(f32[8,768]{1,0:T(8,128)S(1)} %collective-permute-done.1), channel_id=1, source_target_pairs={{0,1},{1,2},{2,3},{3,4},{4,5},{5,6},{6,7},{7,0},{8,9},{9,10},{10,1... | collective-permute-start | bytes 73736 | tf_op jit(solution)/shard_map/ppermute | solution.py:77
  20.8 15.3 %copy-start.5 = (f32[8,768]{1,0:T(8,128)}, f32[8,768]{1,0:T(8,128)S(1)}, u32[]{:S(2)}) copy-start(f32[8,768]{1,0:T(8,128)S(1)} %collective-permute-done.2) | copy-start | bytes 73732
  20.9 5.0 %collective-permute-start.3 = (f32[8,768]{1,0:T(8,128)S(1)}, f32[8,768]{1,0:T(8,128)S(1)}, u32[]{:S(2)}, u32[]{:S(2)}) collective-permute-start(f32[8,768]{1,0:T(8,128)S(1)} %collective-permute-done.2), channel_id=1, source_target_pairs={{0,1},{1,2},{2,3},{3,4},{4,5},{5,6},{6,7},{7,0},{8,9},{9,10},{10,1... | collective-permute-start | bytes 73736 | tf_op jit(solution)/shard_map/ppermute | solution.py:77
  25.9 10.3 %copy-start.6 = (f32[8,768]{1,0:T(8,128)}, f32[8,768]{1,0:T(8,128)S(1)}, u32[]{:S(2)}) copy-start(f32[8,768]{1,0:T(8,128)S(1)} %collective-permute-done.3) | copy-start | bytes 73732
  25.9 5.0 %collective-permute-start.4 = (f32[8,768]{1,0:T(8,128)S(1)}, f32[8,768]{1,0:T(8,128)S(1)}, u32[]{:S(2)}, u32[]{:S(2)}) collective-permute-start(f32[8,768]{1,0:T(8,128)S(1)} %collective-permute-done.3), channel_id=1, source_target_pairs={{0,1},{1,2},{2,3},{3,4},{4,5},{5,6},{6,7},{7,0},{8,9},{9,10},{10,1... | collective-permute-start | bytes 73736 | tf_op jit(solution)/shard_map/ppermute | solution.py:77
  31.0 5.2 %collective-permute-start.5 = (f32[8,768]{1,0:T(8,128)S(1)}, f32[8,768]{1,0:T(8,128)}, u32[]{:S(2)}, u32[]{:S(2)}) collective-permute-start(f32[8,768]{1,0:T(8,128)S(1)} %collective-permute-done.4), channel_id=1, source_target_pairs={{0,1},{1,2},{2,3},{3,4},{4,5},{5,6},{6,7},{7,0},{8,9},{9,10},{10,1... | collective-permute-start | bytes 73736 | tf_op jit(solution)/shard_map/ppermute | solution.py:77
  36.1 13.8 %collective-permute-start.6 = (f32[8,768]{1,0:T(8,128)}, f32[8,768]{1,0:T(8,128)}, u32[]{:S(2)}, u32[]{:S(2)}) collective-permute-start(f32[8,768]{1,0:T(8,128)} %collective-permute-done.5), channel_id=1, source_target_pairs={{0,1},{1,2},{2,3},{3,4},{4,5},{5,6},{6,7},{7,0},{8,9},{9,10},{10,1... | collective-permute-start | bytes 73736 | tf_op jit(solution)/shard_map/ppermute | solution.py:77
  40.4 32.2 %all-to-all-start.1 = ((f32[32,4,768]{2,1,0:T(4,128)}), f32[32,4,768]{2,1,0:T(4,128)S(1)}, u32[]{:S(2)}, u32[]{:S(2)}) async-start(f32[32,4,768]{2,1,0:T(4,128)} %reshape.135), calls=%async_computation.1 | async-start | bytes 786432 | tf_op jit(solution)/shard_map/all_to_all | solution.py:59
  60.3 21.6 %copy-start.2 = (s32[64,8]{0,1:T(8,128)S(1)}, s32[64,8]{0,1:T(8,128)}, u32[]{:S(2)}) copy-start(s32[64,8]{0,1:T(8,128)} %param.12) | copy-start | bytes 6148
  60.3 21.6 %copy-start.9 = (s32[8]{0:T(128)S(1)}, s32[8]{0:T(128)}, u32[]{:S(2)}) copy-start(s32[8]{0:T(128)} %iota_add_fusion) | copy-start | bytes 100
  75.9 91.5 %all-to-all-start.2 = ((f32[32,1,4]{2,1,0:T(1,128)}), f32[32,1,4]{2,1,0:T(1,128)S(1)}, u32[]{:S(2)}, u32[]{:S(2)}) async-start(f32[32,1,4]{2,1,0:T(1,128)} %copy.33), calls=%async_computation.2 | async-start | bytes 32768 | tf_op jit(solution)/shard_map/all_to_all | solution.py:66
  81.9 6.8 %copy-start.1 = (bf16[64,24576]{1,0:T(8,128)(2,1)S(1)}, bf16[64,24576]{1,0:T(8,128)(2,1)}, u32[]{:S(2)}) copy-start(bf16[64,24576]{1,0:T(8,128)(2,1)} %get-tuple-element.124) | copy-start | bytes 9437188 | tf_op jit(solution)/shard_map/while
  92.6 6.8 %copy-start.1 = (bf16[64,24576]{1,0:T(8,128)(2,1)S(1)}, bf16[64,24576]{1,0:T(8,128)(2,1)}, u32[]{:S(2)}) copy-start(bf16[64,24576]{1,0:T(8,128)(2,1)} %get-tuple-element.124) | copy-start | bytes 9437188 | tf_op jit(solution)/shard_map/while
  103.3 6.8 %copy-start.1 = (bf16[64,24576]{1,0:T(8,128)(2,1)S(1)}, bf16[64,24576]{1,0:T(8,128)(2,1)}, u32[]{:S(2)}) copy-start(bf16[64,24576]{1,0:T(8,128)(2,1)} %get-tuple-element.124) | copy-start | bytes 9437188 | tf_op jit(solution)/shard_map/while
  114.0 6.8 %copy-start.1 = (bf16[64,24576]{1,0:T(8,128)(2,1)S(1)}, bf16[64,24576]{1,0:T(8,128)(2,1)}, u32[]{:S(2)}) copy-start(bf16[64,24576]{1,0:T(8,128)(2,1)} %get-tuple-element.124) | copy-start | bytes 9437188 | tf_op jit(solution)/shard_map/while
  146.0 6.8 %copy-start.1 = (bf16[64,24576]{1,0:T(8,128)(2,1)S(1)}, bf16[64,24576]{1,0:T(8,128)(2,1)}, u32[]{:S(2)}) copy-start(bf16[64,24576]{1,0:T(8,128)(2,1)} %get-tuple-element.124) | copy-start | bytes 9437188 | tf_op jit(solution)/shard_map/while
  156.7 6.8 %copy-start.1 = (bf16[64,24576]{1,0:T(8,128)(2,1)S(1)}, bf16[64,24576]{1,0:T(8,128)(2,1)}, u32[]{:S(2)}) copy-start(bf16[64,24576]{1,0:T(8,128)(2,1)} %get-tuple-element.124) | copy-start | bytes 9437188 | tf_op jit(solution)/shard_map/while
  (3 other events, 18.7 us)
